TPU v7x, 256 devices: a whole 4x4x8 slice. The times are simulated.
256 devices in a mesh: dp: 16 (over x, z_hi, core), ctx: 16 (over z_lo, y).
Axes of the slice: x: 4, y: 4, z: 8 (z_hi: 2, z_lo: 4; z = z_hi * 4 + z_lo), core: 2. Of those that a mesh axis runs over, the one named last changes fastest.
Arguments:
- tokens: bfloat16 [16, 4096, 2560], P('dp', 'ctx'), may hold values from -6 to 6
- w_x: bfloat16 [2560, 2560], P(None, 'dp'), may hold values from -0.125 to 0.125
- w_bc: bfloat16 [2560, 256], replicated, may hold values from -0.009765625 to 0.009765625
- w_dt: bfloat16 [2560, 40], replicated, may hold values from -0.125 to 0.125
- dt_bias: float32 [40], replicated, may hold values from -1 to 1
- decay_rate: float32 [40], replicated, may hold values from 0.00012207031 to 0.08
- skip_gain: float32 [40], replicated, may hold values from 0.5 to 1.5
- grad_y: bfloat16 [16, 4096, 2560], P('dp', 'ctx'), may hold values from -6 to 6
Outputs:
- head_out: bfloat16 [16, 4096, 2560], P('dp', 'ctx')
- d_tokens: bfloat16 [16, 4096, 2560], P('dp', 'ctx')
All inputs are finite; a program needn't handle non-finite values.
Results may differ from a plain program's by a relative error of at most 0.017.
Values may be sent and summed in bfloat16 or wider, within the bound.
A program may use at most 128 MiB of HBM per device.

v0:
```python
import jax
import jax.numpy as jnp
from jax import lax
from jax.sharding import PartitionSpec as P

Q = 256
HIGHEST_PRECISION = lax.Precision.HIGHEST


def prefix(value, axis, combine, identity, reverse):
    peers, mine = (lax.axis_size(axis), lax.axis_index(axis))
    everything = jax.tree.map(
        lambda part, kind: lax.all_gather(part.astype(kind), axis),
        value,
        (jnp.bfloat16, jnp.bfloat16),
    )
    start = jax.tree.map(
        lambda part, zero: jnp.broadcast_to(jnp.asarray(zero, part.dtype), part.shape),
        value,
        identity,
    )

    def lap(k, before):
        at = peers - 1 - k if reverse else k
        reached = at > mine if reverse else at < mine
        new = combine(
            before, jax.tree.map(lambda part, own: part[at].astype(own.dtype), everything, value)
        )
        return jax.tree.map(lambda a, b: jnp.where(reached, a, b), new, before)

    return lax.fori_loop(0, peers, lap, start)


def group_rates(raw_block, rate_vec, bias_vec):
    step_size = jax.nn.softplus(raw_block + bias_vec[None, :])
    running = jnp.cumsum(-rate_vec[None, :] * step_size, axis=0)
    return (step_size, running)


def group_forward(entering, pieces, rate_vec, bias_vec, skip_vec):
    x_block, raw_block, b_block, c_block = pieces
    step_size, running = group_rates(raw_block, rate_vec, bias_vec)
    length = x_block.shape[0]
    scores = jnp.dot(
        c_block.astype(jnp.bfloat16),
        b_block.astype(jnp.bfloat16).T,
        preferred_element_type=jnp.float32,
    )
    causal = jnp.arange(length)[:, None] >= jnp.arange(length)[None, :]
    by_head = running.T
    spread = by_head[:, :, None] - by_head[:, None, :]
    decays = jnp.exp(jnp.where(causal[None, :, :], spread, -1e30))
    mixing = scores[None, :, :] * decays * step_size.T[:, None, :]
    within = jnp.einsum("hij,jhp->ihp", mixing, x_block, precision=HIGHEST_PRECISION)
    carried = (
        jnp.einsum("in,hpn->ihp", c_block, entering, precision=HIGHEST_PRECISION)
        * jnp.exp(running)[:, :, None]
    )
    outputs = within + carried + skip_vec[None, :, None] * x_block
    weights_tail = jnp.exp(running[-1][None, :] - running) * step_size
    updated = jnp.exp(running[-1])[:, None, None] * entering + jnp.einsum(
        "jh,jhp,jn->hpn", weights_tail, x_block, b_block, precision=HIGHEST_PRECISION
    )
    return (updated, outputs)


def split_blocks(array, count):
    return array.reshape((count, array.shape[0] // count) + array.shape[1:])


def run_block(values, entering, rate_vec, bias_vec, skip_vec):
    x_all = values[0]
    count = x_all.shape[0] // Q

    def run_advance(carried_in, pieces):
        return group_forward(carried_in, pieces, rate_vec, bias_vec, skip_vec)

    final_state, outputs = lax.scan(
        run_advance, entering, tuple((split_blocks(member, count) for member in values))
    )
    return (outputs.reshape(x_all.shape), final_state)


def block_state(x_all, raw_all, b_all, rate_vec, bias_vec):
    count = x_all.shape[0] // Q

    def block_advance(entering, pieces):
        x_block, raw_block, b_block = pieces
        step_size, running = group_rates(raw_block, rate_vec, bias_vec)
        weights_tail = jnp.exp(running[-1][None, :] - running) * step_size
        updated = jnp.exp(running[-1])[:, None, None] * entering + jnp.einsum(
            "jh,jhp,jn->hpn", weights_tail, x_block, b_block, precision=HIGHEST_PRECISION
        )
        return (updated, running[-1])

    zero_state = jnp.zeros((x_all.shape[1], x_all.shape[2], b_all.shape[1]), jnp.float32)
    final_state, totals = lax.scan(
        block_advance,
        zero_state,
        (split_blocks(x_all, count), split_blocks(raw_all, count), split_blocks(b_all, count)),
    )
    return (jnp.exp(jnp.sum(totals, axis=0)), final_state)


def combine_states(earlier, later):
    return (earlier[0] * later[0], later[0][:, None, None] * earlier[1] + later[1])


def combine_grads(earlier, later):
    return (earlier[0] * later[0], later[1] + later[0][:, None, None] * earlier[1])


def local(tokens, w_x, w_bc, w_dt, dt_bias, decay_rate, skip_gain, grad_y):
    tok_rows = tokens[0]
    steps_here = tok_rows.shape[0]
    head_count = dt_bias.shape[0]
    width_hp = grad_y.shape[2]
    head_size = width_hp // head_count
    state_size = w_bc.shape[1] // 2
    contract = (((1,), (1,)), ((), ()))
    full_panel = lax.all_gather(w_x, "dp", axis=1, tiled=True)
    x_round = jnp.dot(tok_rows, full_panel, preferred_element_type=jnp.float32).astype(jnp.bfloat16)
    bc_round = jnp.dot(tok_rows, w_bc, preferred_element_type=jnp.float32).astype(jnp.bfloat16)
    raw_dt = jnp.dot(tok_rows, w_dt, preferred_element_type=jnp.float32)
    x_float = (
        lax.optimization_barrier(x_round)
        .astype(jnp.float32)
        .reshape(steps_here, head_count, head_size)
    )
    bc_float = lax.optimization_barrier(bc_round).astype(jnp.float32)
    b_float = bc_float[:, :state_size]
    c_float = bc_float[:, state_size:]
    grad_float = grad_y[0].astype(jnp.float32).reshape(steps_here, head_count, head_size)
    decay_total, local_state = block_state(x_float, raw_dt, b_float, decay_rate, dt_bias)
    step_size = jax.nn.softplus(raw_dt + dt_bias[None, :])
    running = jnp.cumsum(-decay_rate[None, :] * step_size, axis=0)
    direct_grad = jnp.einsum(
        "th,thp,tn->hpn", jnp.exp(running), grad_float, c_float, precision=HIGHEST_PRECISION
    )
    unit_decay = jnp.ones_like(decay_total)
    zero_state = jnp.zeros_like(local_state)
    entering = prefix(
        (decay_total, local_state), "ctx", combine_states, (unit_decay, zero_state), False
    )[1]
    later_grad = prefix(
        (decay_total, direct_grad), "ctx", combine_grads, (unit_decay, zero_state), True
    )[1]

    def forward(x_arg, raw_arg, b_arg, c_arg):
        return run_block((x_arg, raw_arg, b_arg, c_arg), entering, decay_rate, dt_bias, skip_gain)

    (head_float, final_state), backward = jax.vjp(forward, x_float, raw_dt, b_float, c_float)
    grad_x, grad_raw, grad_b, grad_c = backward((grad_float, later_grad))
    grad_x_round = grad_x.reshape(steps_here, width_hp).astype(jnp.bfloat16)
    grad_bc_round = jnp.concatenate([grad_b, grad_c], axis=1).astype(jnp.bfloat16)
    grad_raw_round = grad_raw.astype(jnp.bfloat16)
    total = lax.dot_general(grad_x_round, full_panel, contract, preferred_element_type=jnp.float32)
    total = total + lax.dot_general(
        grad_bc_round, w_bc, contract, preferred_element_type=jnp.float32
    )
    total = total + lax.dot_general(
        grad_raw_round, w_dt, contract, preferred_element_type=jnp.float32
    )
    head_out = head_float.reshape(steps_here, width_hp).astype(jnp.bfloat16)
    return (head_out[None], total.astype(jnp.bfloat16)[None])


def solution(mesh):
    placed = (P("dp", "ctx", None), P(None, "dp"), P(), P(), P(), P(), P(), P("dp", "ctx", None))
    return jax.shard_map(
        local,
        mesh=mesh,
        in_specs=placed,
        out_specs=(P("dp", "ctx", None), P("dp", "ctx", None)),
        check_vma=False,
    )
```

profile of v0, /device:TPU:1, one launch (start us, length us, event | category | flops | bytes accessed | tf_op | source)
XLA Modules:
  0.0 483.8 jit_solution(281639778616257343)
XLA Ops:
  10.9 1.8 fusion.51
  12.7 1.6 copy.35
  14.4 2.3 fusion.42
  17.7 39.7 %all-gather.2 = bf16[16,1,40]{2,1,0:T(2,128)(2,1)S(1)} all-gather(bf16[1,1,40]{2,1,0:T(2,128)(2,1)S(1)} %bitcast.230), channel_id=1, replica_groups=mesh['dp'=16,'ctx'=16] {'ctx'}, dimensions={0}, use_global_device_ids=true | all-gather | bytes 1360 | tf_op jit(solution)/shard_map/all_gather | solution.py:13
  57.6 86.7 %all-gather.11.cloned.1.call-done = bf16[640,64,128]{2,1,0:T(8,128)(2,1)} async-done(((bf16[40,64,128]{2,1,0:T(8,128)(2,1)}), bf16[640,64,128]{2,1,0:T(8,128)(2,1)}) %all-gather.11.cloned.1.call-update) | async-done | bytes 10485776 | tf_op jit(solution)/shard_map/all_gather | solution.py:13
  144.3 23.8 %while.23 = (s32[]{:T(128)}, f32[40,64,128]{2,1,0:T(8,128)S(1)}, s32[]{:T(128)}, bf16[16,40,64,128]{3,2,1,0:T(8,128)(2,1)}, bf16[16,40]{1,0:T(8,128)(2,1)S(1)}, ...) while((s32[]{:T(128)}, f32[40,64,128]{2,1,0:T(8,128)S(1)}, s32[]{:T(128)}, ...), condition=%wide.region_5.6_spmd.clone, body=%wide.region_4.5_spmd.clone.sunk | while | flops 1638448 | bytes 3277367 | solution.py:31
  145.7 1.4 fusion.134
  148.7 1.4 fusion.134
  154.6 1.4 fusion.134
  156.1 1.5 fusion.134
  157.6 1.6 fusion.134
  162.2 1.4 fusion.134
  166.6 1.4 fusion.134
  168.0 121.4 %all-gather.7.cloned.1.call-done = bf16[2560,2560]{0,1:T(8,128)(2,1)} async-done(((bf16[2560,160]{0,1:T(8,128)(2,1)}), bf16[2560,2560]{0,1:T(8,128)(2,1)}) %all-gather.7.cloned.1.call-update) | async-done | bytes 13107216 | tf_op jit(solution)/shard_map/all_gather | solution.py:121
  289.5 9.4 %convolution_convert_fusion = bf16[256,2560]{1,0:T(8,128)(2,1)} fusion(bf16[2560,2560]{0,1:T(8,128)(2,1)} %all-gather.7.cloned.1.call-done, bf16[1,256,2560]{2,1,0:T(8,128)(2,1)S(1)} %copy-done), kind=kOutput, calls=%fused_computation.39 | convolution fusion | flops 3356098560 | bytes 15728640 | tf_op jit(solution)/shard_map/dot_general | solution.py:122
  298.8 2.4 copy.34
  301.3 4.1 fusion.30
  305.6 2.3 fusion.41
  307.9 3.0 bitcast_multiply_fusion.2
  311.3 9.3 %fusion.10 = (f32[40,256]{1,0:T(8,128)}, f32[40,256]{1,0:T(8,128)}, f32[40,256]{1,0:T(8,128)}, bf16[256,256]{1,0:T(8,128)(2,1)S(1)}) fusion(f32[40,256]{1,0:T(8,128)S(1)} %get-tuple-element.612, f32[40,256]{1,0:T(8,128)S(1)} %get-tuple-element.610, f32[256,256]{1,0:T(8,128)S(1)} %fusion.76, pred[256,256]{1,0:T(8,128)(4,1)S(1)} %iota_compare_fusion, ...), kind=kOutput, calls=%fused_computation.17 | convolution fusion | flops 369526784 | bytes 3284992 | tf_op jit(solution)/shard_map/transpose(jvp())/while/body/eval_jaxpr/hij,jhp->ihp/dot_general | solution.py:54
  321.1 2.5 fusion.58
  323.7 7.3 %fusion.34 = bf16[256,40,64]{0,2,1:T(8,128)(2,1)S(1)} fusion(bf16[256,40,64]{0,2,1:T(8,128)(2,1)S(1)} %bitcast.214, f32[256,40,64]{0,2,1:T(8,128)S(1)} %copy-done.9, bf16[40,64,256]{2,1,0:T(8,128)(2,1)S(1)} %bitcast.215, f32[40,256]{1,0:T(8,128)S(1)} %copy-done.17, f32[40,256]{1,0:T(8,128)S(1)} %copy-done.15, f32[256,256]{1,0:T(8,128)S(1)} %fusion.76, ...), kind=kOutput, calls=%fused_computation.49 | convolution fusion | flops 2027683840 | bytes 7004320 | tf_op jit(solution)/shard_map/transpose(jvp())/while/body/eval_jaxpr/hij,jhp->ihp/dot_general | solution.py:54
  331.0 5.2 %fusion.111 = f32[256,2560]{1,0:T(8,128)} fusion(bf16[256,2560]{0,1:T(8,128)(2,1)S(1)} %bitcast.223, bf16[2560,2560]{0,1:T(8,128)(2,1)S(1)} %bitcast.211), kind=kOutput, calls=%fused_computation.148 | convolution fusion | flops 3355443200 | bytes 17039360 | tf_op jit(solution)/shard_map/dot_general | solution.py:157
  336.3 89.4 %all-gather.9.cloned.1.call-done = bf16[640,64,128]{2,1,0:T(8,128)(2,1)} async-done(((bf16[40,64,128]{2,1,0:T(8,128)(2,1)}), bf16[640,64,128]{2,1,0:T(8,128)(2,1)}) %all-gather.9.cloned.1.call-update) | async-done | bytes 10485776 | tf_op jit(solution)/shard_map/all_gather | solution.py:13
  425.7 23.3 %while.22 = (s32[]{:T(128)}, f32[40,64,128]{2,1,0:T(8,128)S(1)}, s32[]{:T(128)}, bf16[16,40]{1,0:T(8,128)(2,1)S(1)}, bf16[16,40,64,128]{3,2,1,0:T(8,128)(2,1)}, /*index=5*/s32[]{:T(128)}, s32[]{:T(128)}) while((s32[]{:T(128)}, f32[40,64,128]{2,1,0:T(8,128)S(1)}, s32[]{:T(128)}, bf16[16,40]{1,0:T(8,128)(2,1)S(1)}, ...), condition=%wide.region_3.4_spmd.clone, body=%wide.region_2.3_spmd.clone.sunk | while | flops 1638444 | bytes 3277305 | solution.py:31
  449.0 1.8 multiply_reduce_fusion.1
  450.8 2.8 fusion.35
  454.6 2.5 reduce-window.32
  457.3 10.9 %fusion.29 = bf16[256,40,64]{0,2,1:T(8,128)(2,1)} fusion(bf16[256,40,64]{0,2,1:T(8,128)(2,1)} %bitcast.219, f32[256,40,64]{0,2,1:T(8,128)} %get-tuple-element.617, f32[40,256]{1,0:T(8,128)} %copy-done.16, f32[40,256]{1,0:T(8,128)} %copy-done.14, f32[256,256]{1,0:T(8,128)S(1)} %fusion.76, pred[256,256]{1,0:T(8,128)(4,1)} %copy-done.12, ...), kind=kOutput, calls=%fused_computation.44 | convolution fusion | flops 2027683840 | bytes 5693600 | tf_op jit(solution)/shard_map/jvp()/while/body/eval_jaxpr/hij,jhp->ihp/dot_general | solution.py:54
  468.2 2.4 copy.41
  470.7 4.2 fusion.57
  475.6 1.6 fusion.25
  (141 shorter events, 43.6 us)
Async XLA Ops:
  7.2 1.3 copy-start
  7.2 137.1 %all-gather.11.cloned.1.call-start = ((), (), s32[]{:S(2)}) async-start(), calls=%async_computation.2 | async-start | bytes 11141120 | tf_op jit(solution)/shard_map/all_gather | solution.py:13
  10.0 301.2 %copy-start.16 = (f32[40,256]{1,0:T(8,128)}, f32[40,256]{1,0:T(8,128)S(1)}, u32[]{:S(2)}) copy-start(f32[40,256]{1,0:T(8,128)S(1)} %get-tuple-element.612) | copy-start | bytes 122884
  14.4 3.1 copy-start.3
  16.7 272.8 %all-gather.7.cloned.1.call-start = ((), (), s32[]{:S(2)}) async-start(), calls=%async_computation | async-start | bytes 13926400 | tf_op jit(solution)/shard_map/all_gather | solution.py:121
  17.4 408.3 %all-gather.9.cloned.1.call-start = ((), (), s32[]{:S(2)}) async-start(), calls=%async_computation.1 | async-start | bytes 11141120 | tf_op jit(solution)/shard_map/all_gather | solution.py:13
  17.6 293.7 %copy-start.14 = (f32[40,256]{1,0:T(8,128)}, f32[40,256]{1,0:T(8,128)S(1)}, u32[]{:S(2)}) copy-start(f32[40,256]{1,0:T(8,128)S(1)} %get-tuple-element.610) | copy-start | bytes 122884
  168.0 133.2 %copy-start.1 = (f32[40,64,128]{2,1,0:T(8,128)}, f32[40,64,128]{2,1,0:T(8,128)S(1)}, u32[]{:S(2)}) copy-start(f32[40,64,128]{2,1,0:T(8,128)S(1)} %get-tuple-element.540) | copy-start | bytes 3932164
  301.3 4.3 copy-start.6
  310.9 9.6 %copy-start.12 = (pred[256,256]{1,0:T(8,128)(4,1)}, pred[256,256]{1,0:T(8,128)(4,1)S(1)}, u32[]{:S(2)}) copy-start(pred[256,256]{1,0:T(8,128)(4,1)S(1)} %iota_compare_fusion) | copy-start | bytes 196612
  311.2 9.8 %copy-start.2 = (f32[40,64,128]{2,1,0:T(8,128)S(1)}, f32[40,64,128]{2,1,0:T(8,128)}, u32[]{:S(2)}) copy-start(f32[40,64,128]{2,1,0:T(8,128)} %copy-done.1) | copy-start | bytes 3932164
  311.2 9.8 %copy-start.7 = (bf16[256,2560]{0,1:T(8,128)(2,1)S(1)}, bf16[256,2560]{0,1:T(8,128)(2,1)}, u32[]{:S(2)}) copy-start(bf16[256,2560]{0,1:T(8,128)(2,1)} %copy.34) | copy-start | bytes 3932164
  311.2 12.4 %copy-start.9 = (f32[256,40,64]{0,2,1:T(8,128)S(1)}, f32[256,40,64]{0,2,1:T(8,128)}, u32[]{:S(2)}) copy-start(f32[256,40,64]{0,2,1:T(8,128)} %get-tuple-element.615) | copy-start | bytes 7864324
  311.2 19.7 %slice-start = ((s8[13107200]{0:T(1024)(128)(4,1)}), s8[4194304]{0:T(1024)(128)(4,1)S(1)}, s32[]{:S(2)}) async-start(s8[13107200]{0:T(1024)(128)(4,1)} %bitcast.210), calls=%async_computation.3 | async-start | bytes 8388608
  311.3 19.7 %slice-start.1 = ((s8[13107200]{0:T(1024)(128)(4,1)}), s8[4194304]{0:T(1024)(128)(4,1)S(1)}, s32[]{:S(2)}) async-start(s8[13107200]{0:T(1024)(128)(4,1)} %bitcast.210), calls=%async_computation.4 | async-start | bytes 8388608
  311.3 19.7 %slice-start.2 = ((s8[13107200]{0:T(1024)(128)(4,1)}), s8[4194304]{0:T(1024)(128)(4,1)S(1)}, s32[]{:S(2)}) async-start(s8[13107200]{0:T(1024)(128)(4,1)} %bitcast.210), calls=%async_computation.5 | async-start | bytes 8388608
  320.6 3.0 copy-start.4
  320.6 3.0 copy-start.15
  320.6 3.1 copy-start.17
  320.6 3.1 copy-start.19
  320.6 3.1 copy-start.13
  323.7 7.3 %slice-start.3 = ((s8[13107200]{0:T(1024)(128)(4,1)}), s8[524288]{0:T(1024)(128)(4,1)S(1)}, s32[]{:S(2)}) async-start(s8[13107200]{0:T(1024)(128)(4,1)} %bitcast.210), calls=%async_computation.6 | async-start | bytes 1048576
  449.0 1.8 copy-start.5
  470.7 4.3 copy-start.11
  470.7 4.3 copy-start.18
  470.7 4.9 %copy-start.8 = (f32[256,2560]{1,0:T(8,128)S(1)}, f32[256,2560]{1,0:T(8,128)}, u32[]{:S(2)}) copy-start(f32[256,2560]{1,0:T(8,128)} %fusion.111) | copy-start | bytes 7864324
  470.7 4.9 %copy-start.10 = (bf16[2560,256]{1,0:T(8,128)(2,1)S(1)}, bf16[2560,256]{1,0:T(8,128)(2,1)}, u32[]{:S(2)}) copy-start(bf16[2560,256]{1,0:T(8,128)(2,1)} %param.14) | copy-start | bytes 3932164
Sparse Core Ops, SparseCore 0:
  16.8 127.4 all-gather.10
  147.0 142.4 all-gather.6
  308.0 117.6 all-gather.8
where the time goes:
time: 486 us; the launch traced here: 484 us
  waiting for transfers between devices  298 us (61%)
  matrix products  66.4 us (14%)
  other arithmetic  56.4 us (12%)
  blocking collectives  39.7 us (8%)
  between operations  14.2 us (3%)
  local copies, waits for them, and re-layouts  7.68 us (2%)
    all_gather x2, waiting for transfers between devices, prefix(): lax.all_gather(part.astype(kind), axis)  176 us
    all_gather x1, waiting for transfers between devices, local(): full_panel = lax.all_gather(w_x, 'dp', axis=1, tiled=True)  121 us
    select_n x32, other arithmetic, lap(): return jax.tree.map(lambda a, b: jnp.where(reached, a, b), new, before)  45.6 us
    all_gather x1, blocking collectives, prefix(): lax.all_gather(part.astype(kind), axis)  39.7 us
    dot_general x3, matrix products, group_forward(): jnp.einsum('hij,jhp->ihp', mixing, x_block, precision=HIGHEST_PRECISION)  27.5 us
  transfers between devices with their start and end apart: 3, of which 3 were waited for; matrix products, arithmetic and copies ran while one was open for 11% of the time, Pallas kernels for 0%

commit v1 on v0

--- a/solution.py
+++ b/solution.py
@@ -5,6 +5,16 @@
 
 Q = 256
 HIGHEST_PRECISION = lax.Precision.HIGHEST
+
+
+def wait_body(shard_in, which_axis):
+    lower = jnp.concatenate(
+        lax.all_to_all(
+            jnp.stack([shard_in for _ in range(lax.axis_size(which_axis))]), which_axis, 0, 0
+        ),
+        1,
+    )
+    return lower
 
 
 def prefix(value, axis, combine, identity, reverse):
@@ -118,7 +128,7 @@
     head_size = width_hp // head_count
     state_size = w_bc.shape[1] // 2
     contract = (((1,), (1,)), ((), ()))
-    full_panel = lax.all_gather(w_x, "dp", axis=1, tiled=True)
+    full_panel = wait_body(w_x, "dp")
     x_round = jnp.dot(tok_rows, full_panel, preferred_element_type=jnp.float32).astype(jnp.bfloat16)
     bc_round = jnp.dot(tok_rows, w_bc, preferred_element_type=jnp.float32).astype(jnp.bfloat16)
     raw_dt = jnp.dot(tok_rows, w_dt, preferred_element_type=jnp.float32)

time: 486 us -> 683 us (1.41)
  blocking collectives: 39.7 us -> 404 us
  waiting for transfers between devices: 298 us -> 103 us
  starting transfers between devices: 0.12 us -> 12.5 us
  local copies, waits for them, and re-layouts: 7.68 us -> 16.4 us
  other arithmetic: 56.4 us -> 64.6 us
    all_gather x1, blocking collectives: 39.7 us -> 404 us  [prefix(): lax.all_gather(part.astype(kind), axis)]
    all_gather x1 -> x0, waiting for transfers between devices: 121 us -> none  [local(): full_panel = lax.all_gather(w_x, 'dp', axis=1, tiled=True)]
    all_gather x2, waiting for transfers between devices: 176 us -> 103 us  [prefix(): lax.all_gather(part.astype(kind), axis)]
    all_to_all x0 -> x1, starting transfers between devices: none -> 12.4 us  [wait_body(): lax.all_to_all(jnp.stack([shard_in for _ in range(lax.axis_size(which_axi...]
    convert_element_type x32, other arithmetic: 0.34 us -> 10.7 us  [lap(): part[at].astype(own.dtype)]
    another operation x5 -> x6, local copies, waits for them, and re-layouts: 0.26 us -> 7.41 us  [the longest x1 7.15 us: wait_body(): jnp.stack([shard_in for _ in range(lax.axis_size(which_axis))])]
  transfers between devices with their start and end apart: 3 -> 3, of which waited for: 3 -> 1; matrix products, arithmetic and copies ran while one was open for 11% -> 9% of each run, Pallas kernels for 0% -> 0%
where the time goes in v1:
time: 683 us; the launch traced here: 681 us
  blocking collectives  404 us (59%)
  waiting for transfers between devices  103 us (15%)
  matrix products  65.1 us (10%)
  other arithmetic  64.6 us (9%)
  local copies, waits for them, and re-layouts  16.4 us (2%)
  between operations  14.7 us (2%)
  starting transfers between devices  12.5 us (2%)
    all_gather x1, blocking collectives, prefix(): lax.all_gather(part.astype(kind), axis)  404 us
    all_gather x2, waiting for transfers between devices, prefix(): lax.all_gather(part.astype(kind), axis)  103 us
    select_n x32, other arithmetic, lap(): return jax.tree.map(lambda a, b: jnp.where(reached, a, b), new, before)  45.7 us
    dot_general x3, matrix products, group_forward(): jnp.einsum('hij,jhp->ihp', mixing, x_block, precision=HIGHEST_PRECISION)  25.8 us
  transfers between devices with their start and end apart: 3, of which 1 were waited for; matrix products, arithmetic and copies ran while one was open for 9% of the time, Pallas kernels for 0%

profile of v1, /device:TPU:1, one launch (start us, length us, event | category | flops | bytes accessed | tf_op | source)
XLA Modules:
  0.0 680.9 jit_solution(4434538527779282627)
XLA Ops:
  7.3 1.7 copy.36
  11.1 1.8 fusion.51
  12.9 2.3 fusion.42
  15.2 7.2 %stack.2 = bf16[16,2560,160]{1,2,0:T(8,128)(2,1)} broadcast(bf16[2560,160]{0,1:T(8,128)(2,1)} %param.13), dimensions={1,2} | broadcast | bytes 13926400 | tf_op jit(solution)/shard_map/stack | solution.py:13
  22.4 12.4 %all-to-all-start = ((bf16[16,2560,160]{1,2,0:T(8,128)(2,1)}), bf16[16,2560,160]{1,2,0:T(8,128)(2,1)}, u32[]{:S(2)}, u32[]{:S(2)}) async-start(bf16[16,2560,160]{1,2,0:T(8,128)(2,1)} %stack.2), calls=%async_computation | async-start | bytes 26214400 | tf_op jit(solution)/shard_map/all_to_all | solution.py:12
  35.7 403.9 %all-gather.2 = bf16[16,1,40]{2,1,0:T(2,128)(2,1)S(1)} all-gather(bf16[1,1,40]{2,1,0:T(2,128)(2,1)S(1)} %bitcast.231), channel_id=1, replica_groups=mesh['dp'=16,'ctx'=16] {'ctx'}, dimensions={0}, use_global_device_ids=true | all-gather | bytes 1360 | tf_op jit(solution)/shard_map/all_gather | solution.py:23
  439.9 23.7 %while.23 = (s32[]{:T(128)}, f32[40,64,128]{2,1,0:T(8,128)S(1)}, s32[]{:T(128)}, bf16[16,40,64,128]{3,2,1,0:T(8,128)(2,1)}, bf16[16,40]{1,0:T(8,128)(2,1)S(1)}, ...) while((s32[]{:T(128)}, f32[40,64,128]{2,1,0:T(8,128)S(1)}, s32[]{:T(128)}, ...), condition=%wide.region_5.6_spmd.clone, body=%wide.region_4.5_spmd.clone.sunk | while | flops 1638448 | bytes 3277375 | solution.py:41
  439.9 1.4 fusion.134
  441.4 1.4 fusion.134
  442.9 1.4 fusion.134
  444.4 1.4 fusion.134
  447.3 1.4 fusion.134
  450.3 1.4 fusion.134
  454.7 1.4 fusion.134
  459.2 1.4 fusion.134
  463.6 9.8 %convolution_convert_fusion = bf16[256,2560]{1,0:T(8,128)(2,1)} fusion(bf16[2560,2560]{0,1:T(8,128)(2,1)} %bitcast.3, bf16[1,256,2560]{2,1,0:T(8,128)(2,1)S(1)} %copy-done), kind=kOutput, calls=%fused_computation.39 | convolution fusion | flops 3356098560 | bytes 15728640 | tf_op jit(solution)/shard_map/dot_general | solution.py:132
  473.4 1.6 copy.35
  476.1 2.7 fusion.30
  479.6 3.6 fusion.41
  483.2 1.7 bitcast_multiply_fusion.2
  485.9 10.0 %fusion.10 = (f32[40,256]{1,0:T(8,128)}, f32[40,256]{1,0:T(8,128)}, f32[40,256]{1,0:T(8,128)}, bf16[256,256]{1,0:T(8,128)(2,1)S(1)}) fusion(f32[40,256]{1,0:T(8,128)} %get-tuple-element.612, f32[40,256]{1,0:T(8,128)} %get-tuple-element.610, f32[256,256]{1,0:T(8,128)S(1)} %fusion.76, pred[256,256]{1,0:T(8,128)(4,1)S(1)} %iota_compare_fusion, ...), kind=kOutput, calls=%fused_computation.17 | convolution fusion | flops 369526784 | bytes 3284992 | tf_op jit(solution)/shard_map/transpose(jvp())/while/body/eval_jaxpr/hij,jhp->ihp/dot_general | solution.py:64
  496.4 2.5 fusion.58
  499.0 7.3 %fusion.34 = bf16[256,40,64]{0,2,1:T(8,128)(2,1)S(1)} fusion(bf16[256,40,64]{0,2,1:T(8,128)(2,1)S(1)} %bitcast.216, f32[256,40,64]{0,2,1:T(8,128)S(1)} %copy-done.12, bf16[40,64,256]{2,1,0:T(8,128)(2,1)S(1)} %bitcast.217, f32[40,256]{1,0:T(8,128)S(1)} %copy-done.28, f32[40,256]{1,0:T(8,128)S(1)} %copy-done.26, f32[256,256]{1,0:T(8,128)S(1)} %copy-done.16, ...), kind=kOutput, calls=%fused_computation.49 | convolution fusion | flops 2027683840 | bytes 7004320 | tf_op jit(solution)/shard_map/transpose(jvp())/while/body/eval_jaxpr/hij,jhp->ihp/dot_general | solution.py:64
  506.3 8.1 %fusion.111 = f32[256,2560]{1,0:T(8,128)} fusion(bf16[256,2560]{0,1:T(8,128)(2,1)S(1)} %bitcast.224, bf16[2560,2560]{0,1:T(8,128)(2,1)} %bitcast.3), kind=kOutput, calls=%fused_computation.148 | convolution fusion | flops 3355443200 | bytes 17039360 | tf_op jit(solution)/shard_map/dot_general | solution.py:167
  514.4 102.6 %all-gather.6.cloned.1.call-done = bf16[640,64,128]{2,1,0:T(8,128)(2,1)} async-done(((bf16[40,64,128]{2,1,0:T(8,128)(2,1)}), bf16[640,64,128]{2,1,0:T(8,128)(2,1)}) %all-gather.6.cloned.1.call-update) | async-done | bytes 10485776 | tf_op jit(solution)/shard_map/all_gather | solution.py:23
  617.1 33.6 %while.22 = (s32[]{:T(128)}, f32[40,64,128]{2,1,0:T(8,128)S(1)}, s32[]{:T(128)}, bf16[16,40]{1,0:T(8,128)(2,1)}, bf16[16,40,64,128]{3,2,1,0:T(8,128)(2,1)}, /*index=5*/s32[]{:T(128)}, s32[]{:T(128)}) while((s32[]{:T(128)}, f32[40,64,128]{2,1,0:T(8,128)S(1)}, s32[]{:T(128)}, bf16[16,40]{1,0:T(8,128)(2,1)}, ...), condition=%wide.region_3.4_spmd.clone, body=%wide.region_2.3_spmd.clone.sunk | while | flops 1638444 | bytes 3277313 | solution.py:41
  650.7 2.6 fusion.35
  654.6 8.6 %fusion.29 = bf16[256,40,64]{0,2,1:T(8,128)(2,1)S(1)} fusion(bf16[256,40,64]{0,2,1:T(8,128)(2,1)S(1)} %bitcast.222, f32[256,40,64]{0,2,1:T(8,128)S(1)} %get-tuple-element.617, f32[40,256]{1,0:T(8,128)S(1)} %copy-done.29, f32[40,256]{1,0:T(8,128)S(1)} %copy-done.27, f32[256,256]{1,0:T(8,128)S(1)} %copy-done.17, pred[256,256]{1,0:T(8,128)(4,1)S(1)} %copy-done.23, ...), kind=kOutput, calls=%fused_computation.44 | convolution fusion | flops 2027683840 | bytes 5693600 | tf_op jit(solution)/shard_map/jvp()/while/body/eval_jaxpr/hij,jhp->ihp/dot_general | solution.py:64
  663.3 1.6 copy.42
  665.2 2.8 reduce-window.32
  669.8 2.5 fusion.57
  672.4 1.7 fusion.25
  (176 shorter events, 54.9 us)
Async XLA Ops:
  7.2 432.6 %all-gather.8.cloned.1.call-start = ((), (), s32[]{:S(2)}) async-start(), calls=%async_computation.2 | async-start | bytes 11141120 | tf_op jit(solution)/shard_map/all_gather | solution.py:23
  9.0 6.2 copy-start.4
  11.0 467.8 %copy-start.31 = (f32[40,2]{0,1:T(2,128)}, f32[40,2]{0,1:T(2,128)S(1)}, u32[]{:S(2)}) copy-start(f32[40,2]{0,1:T(2,128)S(1)} %slice.47) | copy-start | bytes 964
  22.4 441.2 %all-to-all-start = ((bf16[16,2560,160]{1,2,0:T(8,128)(2,1)}), bf16[16,2560,160]{1,2,0:T(8,128)(2,1)}, u32[]{:S(2)}, u32[]{:S(2)}) async-start(bf16[16,2560,160]{1,2,0:T(8,128)(2,1)} %stack.2), calls=%async_computation | async-start | bytes 26214400 | tf_op jit(solution)/shard_map/all_to_all | solution.py:12
  34.8 582.3 %all-gather.6.cloned.1.call-start = ((), (), s32[]{:S(2)}) async-start(), calls=%async_computation.1 | async-start | bytes 11141120 | tf_op jit(solution)/shard_map/all_gather | solution.py:23
  439.8 38.9 %copy-start.33 = (f32[40]{0:T(128)}, f32[40]{0:T(128)S(1)}, u32[]{:S(2)}) copy-start(f32[40]{0:T(128)S(1)} %slice_reduce_fusion.2) | copy-start | bytes 484
  463.6 9.9 %copy-start.35 = (bf16[16,40]{1,0:T(8,128)(2,1)}, bf16[16,40]{1,0:T(8,128)(2,1)S(1)}, u32[]{:S(2)}) copy-start(bf16[16,40]{1,0:T(8,128)(2,1)S(1)} %get-tuple-element.738) | copy-start | bytes 3844
  463.6 11.5 %copy-start.2 = (f32[40,64,128]{2,1,0:T(8,128)}, f32[40,64,128]{2,1,0:T(8,128)S(1)}, u32[]{:S(2)}) copy-start(f32[40,64,128]{2,1,0:T(8,128)S(1)} %get-tuple-element.540) | copy-start | bytes 3932164
  478.8 4.4 copy-start.5
  479.6 5.4 copy-start.19
  485.0 10.9 %copy-start.22 = (pred[256,256]{1,0:T(8,128)(4,1)}, pred[256,256]{1,0:T(8,128)(4,1)S(1)}, u32[]{:S(2)}) copy-start(pred[256,256]{1,0:T(8,128)(4,1)S(1)} %iota_compare_fusion) | copy-start | bytes 196612
  485.2 10.7 %copy-start.15 = (f32[256,256]{1,0:T(8,128)}, f32[256,256]{1,0:T(8,128)S(1)}, u32[]{:S(2)}) copy-start(f32[256,256]{1,0:T(8,128)S(1)} %fusion.76) | copy-start | bytes 786436
  485.9 10.5 %copy-start.3 = (f32[40,64,128]{2,1,0:T(8,128)S(1)}, f32[40,64,128]{2,1,0:T(8,128)}, u32[]{:S(2)}) copy-start(f32[40,64,128]{2,1,0:T(8,128)} %copy-done.2) | copy-start | bytes 3932164
  485.9 10.5 %copy-start.8 = (bf16[256,2560]{0,1:T(8,128)(2,1)S(1)}, bf16[256,2560]{0,1:T(8,128)(2,1)}, u32[]{:S(2)}) copy-start(bf16[256,2560]{0,1:T(8,128)(2,1)} %copy-done.7) | copy-start | bytes 3932164
  485.9 10.5 %copy-start.20 = (f32[256,40]{0,1:T(8,128)S(1)}, f32[256,40]{0,1:T(8,128)}, u32[]{:S(2)}) copy-start(f32[256,40]{0,1:T(8,128)} %copy-done.19) | copy-start | bytes 122884
  485.9 13.0 %copy-start.12 = (f32[256,40,64]{0,2,1:T(8,128)S(1)}, f32[256,40,64]{0,2,1:T(8,128)}, u32[]{:S(2)}) copy-start(f32[256,40,64]{0,2,1:T(8,128)} %get-tuple-element.615) | copy-start | bytes 7864324
  495.9 3.1 copy-start.6
  495.9 3.1 copy-start.26
  495.9 3.1 copy-start.28
  495.9 3.1 copy-start.40
  495.9 3.1 copy-start.16
  495.9 3.1 copy-start.23
  663.2 1.8 copy-start.18
  663.2 1.8 copy-start.21
  663.2 1.8 copy-start.24
  663.2 1.8 copy-start.25
  663.2 4.8 copy-start.30
  663.2 4.8 copy-start.34
  663.3 4.8 copy-start.37
  668.7 3.6 copy-start.11
  668.7 3.6 copy-start.13
  669.8 4.2 copy-start.1
  (13 other events, 19.6 us)
Sparse Core Ops, SparseCore 0:
  15.3 271.8 all-gather.7
  483.3 133.7 all-gather.5
